TPU v7x, 256 devices: a whole 4x4x8 slice. The times are simulated.
256 devices in a mesh: row: 8 (over y, core), col: 32 (over x, z).
Axes of the slice: x: 4, y: 4, z: 8, core: 2. Of those that a mesh axis runs over, the one named last changes fastest.
Arguments:
- tokens: bfloat16 [2048, 6144], P('row', 'col'), may hold values from -6 to 6
- cotangent: bfloat16 [2048, 6144], P('row', 'col'), may hold values from -6 to 6
- w_expand: bfloat16 [6144, 12288], P('row', 'col'), may hold values from -0.078125 to 0.078125
- w_reduce: bfloat16 [6144, 12288], P('row', 'col'), may hold values from -0.0546875 to 0.0546875
- expand_mean: bfloat16 [6144, 12288], P('row', 'col'), may hold values from -1 to 1
- expand_mean_scale: float32 [24, 12288], P('row', 'col'), may hold values from 4 to 16
- expand_var: bfloat16 [6144, 12288], P('row', 'col'), may hold values from 0.049804688 to 1
- expand_var_scale: float32 [24, 12288], P('row', 'col'), may hold values from 4 to 16
- reduce_mean: bfloat16 [6144, 12288], P('row', 'col'), may hold values from -1 to 1
- reduce_mean_scale: float32 [24, 12288], P('row', 'col'), may hold values from 4 to 16
- reduce_var: bfloat16 [6144, 12288], P('row', 'col'), may hold values from 0.049804688 to 1
- reduce_var_scale: float32 [24, 12288], P('row', 'col'), may hold values from 4 to 16
Outputs:
- grad_tokens: bfloat16 [2048, 6144], P('row', 'col')
- new_expand: bfloat16 [6144, 12288], P('row', 'col')
- expand_mean_next: bfloat16 [6144, 12288], P('row', 'col')
- expand_mean_scale_next: float32 [24, 12288], P('row', 'col')
- expand_var_next: bfloat16 [6144, 12288], P('row', 'col')
- expand_var_scale_next: float32 [24, 12288], P('row', 'col')
- new_reduce: bfloat16 [6144, 12288], P('row', 'col')
- reduce_mean_next: bfloat16 [6144, 12288], P('row', 'col')
- reduce_mean_scale_next: float32 [24, 12288], P('row', 'col')
- reduce_var_next: bfloat16 [6144, 12288], P('row', 'col')
- reduce_var_scale_next: float32 [24, 12288], P('row', 'col')
All inputs are finite; a program needn't handle non-finite values.
Results may differ from a plain program's by a relative error of at most 0.0049.
Values may be sent and summed in bfloat16 or wider, within the bound.
No kernel may reach another device: no remote copies, remote signals or barrier semaphores. Data moves between devices by JAX's collectives and lax.ppermute only.
A program may use at most 128 MiB of HBM per device.

v0:
```python
import jax
import jax.numpy as jnp
from jax import lax
from jax.sharding import PartitionSpec as P

STEP = 10
beta_one = 0.9
beta_two = 0.999
adam_eps = 1e-08
learn_rate = 0.001
decay_rate = 0.1
scale_eps = 1e-06


def gelu_pair(pre_act):
    cdf_part = 0.5 * (1.0 + lax.erf(pre_act * 0.7071067811865476))
    slope = cdf_part + pre_act * jnp.exp(-0.5 * pre_act * pre_act) * 0.3989422804014327
    return (pre_act * cdf_part, slope)


def spread_scale(values, scale):
    blocks = scale.shape[0]
    shaped = values.reshape(blocks, values.shape[0] // blocks, values.shape[1])
    return (shaped * scale[:, None, :]).reshape(values.shape)


def block_max(values, blocks):
    shaped = values.reshape(blocks, values.shape[0] // blocks, values.shape[1])
    return jnp.max(jnp.abs(shaped), axis=1) + scale_eps


def adam_step(weight, grad_w, mean_q, mean_scale, var_q, var_scale):
    blocks = mean_scale.shape[0]
    mean_new = (
        beta_one * spread_scale(mean_q.astype(jnp.float32), mean_scale) + (1.0 - beta_one) * grad_w
    )
    var_new = (
        beta_two * spread_scale(var_q.astype(jnp.float32), var_scale)
        + (1.0 - beta_two) * grad_w * grad_w
    )
    mean_hat = mean_new / (1.0 - beta_one**STEP)
    var_hat = var_new / (1.0 - beta_two**STEP)
    old_weight = weight.astype(jnp.float32)
    new_weight = (
        old_weight
        - learn_rate * (mean_hat / (jnp.sqrt(var_hat) + adam_eps) + decay_rate * old_weight)
    ).astype(jnp.bfloat16)
    mean_scale_next = block_max(mean_new, blocks)
    var_scale_next = block_max(var_new, blocks)
    mean_next = spread_scale(mean_new, 1.0 / mean_scale_next).astype(jnp.bfloat16)
    var_next = spread_scale(var_new, 1.0 / var_scale_next).astype(jnp.bfloat16)
    return (new_weight, mean_next, mean_scale_next, var_next, var_scale_next)


def contract_first(left, right):
    return lax.dot_general(
        left, right, (((0,), (0,)), ((), ())), preferred_element_type=jnp.float32
    )


def local(
    tokens,
    cotangent,
    w_expand,
    w_reduce,
    expand_mean,
    expand_mean_scale,
    expand_var,
    expand_var_scale,
    reduce_mean,
    reduce_mean_scale,
    reduce_var,
    reduce_var_scale,
):
    token_rows, cot_rows = (
        lax.all_gather(tokens, "col", axis=1, tiled=True),
        lax.all_gather(cotangent, "col", axis=1, tiled=True),
    )
    input_whole, cot_whole = (
        lax.all_to_all(token_rows, "row", split_axis=1, concat_axis=0, tiled=True),
        lax.all_to_all(cot_rows, "row", split_axis=1, concat_axis=0, tiled=True),
    )
    up_panel, down_panel = (
        lax.all_gather(w_expand, "row", axis=0, tiled=True),
        lax.all_gather(w_reduce, "row", axis=0, tiled=True),
    )
    pre_act = jnp.dot(token_rows, up_panel, preferred_element_type=jnp.float32)
    act_grad = jnp.dot(cot_rows, down_panel, preferred_element_type=jnp.float32)
    activated, slope = gelu_pair(pre_act)
    activated = activated.astype(jnp.bfloat16)
    pre_grad = (act_grad * slope).astype(jnp.bfloat16)
    grad_cols = lax.psum_scatter(
        lax.dot_general(
            up_panel, pre_grad, (((1,), (1,)), ((), ())), preferred_element_type=jnp.float32
        ),
        "col",
        scatter_dimension=0,
        tiled=True,
    )
    grad_tokens = grad_cols.T.astype(jnp.bfloat16)
    grad_expand = contract_first(input_whole, lax.all_gather(pre_grad, "row", axis=0, tiled=True))
    grad_reduce = contract_first(cot_whole, lax.all_gather(activated, "row", axis=0, tiled=True))
    first = adam_step(
        w_expand, grad_expand, expand_mean, expand_mean_scale, expand_var, expand_var_scale
    )
    second = adam_step(
        w_reduce, grad_reduce, reduce_mean, reduce_mean_scale, reduce_var, reduce_var_scale
    )
    return (
        grad_tokens,
        first[0],
        first[1],
        first[2],
        first[3],
        first[4],
        second[0],
        second[1],
        second[2],
        second[3],
        second[4],
    )


def solution(mesh):
    placed = (
        P("row", "col"),
        P("row", "col"),
        P("row", "col"),
        P("row", "col"),
        P("row", "col"),
        P("row", "col"),
        P("row", "col"),
        P("row", "col"),
        P("row", "col"),
        P("row", "col"),
        P("row", "col"),
        P("row", "col"),
    )
    return jax.shard_map(
        local,
        mesh=mesh,
        in_specs=placed,
        out_specs=(
            P("row", "col"),
            P("row", "col"),
            P("row", "col"),
            P("row", "col"),
            P("row", "col"),
            P("row", "col"),
            P("row", "col"),
            P("row", "col"),
            P("row", "col"),
            P("row", "col"),
            P("row", "col"),
        ),
        check_vma=False,
    )
```

profile of v0, /device:TPU:8, one launch (start us, length us, event | category | flops | bytes accessed | tf_op | source)
XLA Modules:
  0.0 555.6 jit_solution(1710327823756502407)
XLA Ops:
  10.0 82.9 %all-gather.11.cloned.1.call-done = bf16[256,6144]{0,1:T(8,128)(2,1)} async-done(((bf16[256,192]{0,1:T(8,128)(2,1)}), bf16[256,6144]{0,1:T(8,128)(2,1)}) %all-gather.11.cloned.1.call-update) | async-done | bytes 3145744 | tf_op jit(solution)/shard_map/all_gather | solution.py:76
  92.9 34.3 %all-gather.13.cloned.1.call-done = bf16[6144,384]{1,0:T(8,128)(2,1)} async-done(((bf16[768,384]{1,0:T(8,128)(2,1)}), bf16[6144,384]{1,0:T(8,128)(2,1)}) %all-gather.13.cloned.1.call-update) | async-done | bytes 4718608 | tf_op jit(solution)/shard_map/all_gather | solution.py:84
  127.2 5.8 %multiply_convert_fusion.4 = (bf16[256,384]{1,0:T(8,128)(2,1)}, f32[256,384]{1,0:T(8,128)S(1)}) fusion(bf16[256,6144]{0,1:T(8,128)(2,1)} %all-gather.11.cloned.1.call-done, bf16[6144,384]{1,0:T(8,128)(2,1)} %all-gather.13.cloned.1.call-done), kind=kOutput, calls=%fused_computation.30 | convolution fusion | flops 1208451072 | bytes 8454144 | tf_op jit(solution)/shard_map/dot_general | solution.py:87
  133.1 77.2 %all-gather.7.cloned.1.call-done = bf16[256,6144]{0,1:T(8,128)(2,1)} async-done(((bf16[256,192]{0,1:T(8,128)(2,1)}), bf16[256,6144]{0,1:T(8,128)(2,1)}) %all-gather.7.cloned.1.call-update) | async-done | bytes 3145744 | tf_op jit(solution)/shard_map/all_gather | solution.py:77
  210.2 34.2 %all-gather.9.cloned.1.call-done = bf16[6144,384]{1,0:T(8,128)(2,1)} async-done(((bf16[768,384]{1,0:T(8,128)(2,1)}), bf16[6144,384]{1,0:T(8,128)(2,1)}) %all-gather.9.cloned.1.call-update) | async-done | bytes 4718608 | tf_op jit(solution)/shard_map/all_gather | solution.py:85
  244.4 5.9 %fusion.8 = bf16[256,384]{1,0:T(8,128)(2,1)} fusion(bf16[256,6144]{0,1:T(8,128)(2,1)} %all-gather.7.cloned.1.call-done, bf16[6144,384]{1,0:T(8,128)(2,1)} %all-gather.9.cloned.1.call-done, f32[256,384]{1,0:T(8,128)S(1)} %get-tuple-element.82), kind=kOutput, calls=%fused_computation.24 | convolution fusion | flops 1208942592 | bytes 8454144 | tf_op jit(solution)/shard_map/dot_general | solution.py:88
  250.9 7.0 %convolution_bitcast_fusion = f32[6144,256]{0,1:T(8,128)} fusion(bf16[256,384]{1,0:T(8,128)(2,1)} %fusion.8, bf16[6144,384]{1,0:T(8,128)(2,1)} %all-gather.13.cloned.1.call-done), kind=kOutput, calls=%fused_computation | convolution fusion | flops 1207959552 | bytes 11206656 | tf_op jit(solution)/shard_map/dot_general | solution.py:93
  257.9 6.6 %copy.123 = f32[6144,256]{1,0:T(8,128)} copy(f32[6144,256]{0,1:T(8,128)} %convolution_bitcast_fusion) | data formatting | bytes 12582912
  266.4 49.7 %all_to_all.38 = bf16[256,8,768]{0,2,1:T(8,128)(2,1)} all-to-all(bf16[256,8,768]{0,2,1:T(8,128)(2,1)S(1)} %bitcast.38), channel_id=1, replica_groups=mesh['row'=8,'col'=32] {'row'}, dimensions={1} | all-to-all | bytes 6291456 | tf_op jit(solution)/shard_map/all_to_all | solution.py:80
  316.1 4.0 all-to-all-start.1
  320.2 2.1 copy.96
  325.5 2.7 copy.101
  329.3 2.7 copy.98
  332.0 2.1 copy.100
  337.4 2.7 copy.108
  341.2 2.7 copy.111
  343.8 2.1 copy.107
  346.0 2.1 copy.110
  348.1 4.7 copy.99
  352.8 4.3 all-to-all-done.1
  357.1 2.9 copy.109
  360.0 6.3 %fusion.18 = (f32[768,384]{0,1:T(8,128)}, f32[768,384]{0,1:T(8,128)S(1)}, f32[768,384]{0,1:T(8,128)S(1)}, f32[768,384]{0,1:T(8,128)S(1)}) fusion(f32[768,384]{0,1:T(8,128)} %copy.98, bf16[768,384]{0,1:T(8,128)(2,1)} %copy.97, f32[768,384]{0,1:T(8,128)} %copy.101, bf16[768,384]{0,1:T(8,128)(2,1)} %copy.100, ...), kind=kOutput, calls=%fused_computation.44 | convolution fusion | flops 1211793408 | bytes 12976128 | tf_op jit(solution)/shard_map/dot_general | solution.py:56
  366.3 2.7 copy.102
  377.8 2.7 copy.105
  380.5 3.5 multiply_convert_fusion.2
  384.0 2.3 copy.117
  388.4 2.1 copy.119
  390.5 6.4 %fusion.15 = (f32[768,384]{0,1:T(8,128)}, f32[768,384]{0,1:T(8,128)}, f32[768,384]{0,1:T(8,128)}, f32[768,384]{0,1:T(8,128)}) fusion(f32[768,384]{0,1:T(8,128)} %copy.108, bf16[768,384]{0,1:T(8,128)(2,1)} %copy.107, f32[768,384]{0,1:T(8,128)} %copy.111, bf16[768,384]{0,1:T(8,128)(2,1)} %copy.110, bf16[2048,384]{1,0:T(8,128)(2,1)} %all-gather.17.cloned.1.call-done, ...), kind=kOutput, calls=%fused_computation.42 | convolution fusion | flops 1211793408 | bytes 12976128 | tf_op jit(solution)/shard_map/dot_general | solution.py:56
  402.5 2.9 copy.115
  405.4 3.5 multiply_convert_fusion
  408.9 2.2 copy.120
  413.2 133.7 %reduce-scatter.4.cloned.1.call-done = f32[192,256]{1,0:T(8,128)} async-done(((f32[6144,256]{1,0:T(8,128)}), f32[192,256]{1,0:T(8,128)}) %reduce-scatter.4.cloned.1.call-update) | async-done | bytes 196624
  (66 shorter events, 34.4 us)
Async XLA Ops:
  7.2 85.7 %all-gather.11.cloned.1.call-start = ((), (), s32[]{:S(2)}) async-start(), calls=%async_computation.5 | async-start | bytes 3244032 | tf_op jit(solution)/shard_map/all_gather | solution.py:76
  7.9 119.3 %all-gather.13.cloned.1.call-start = ((), (), s32[]{:S(2)}) async-start(), calls=%async_computation.6 | async-start | bytes 5308416 | tf_op jit(solution)/shard_map/all_gather | solution.py:84
  8.7 201.6 %all-gather.7.cloned.1.call-start = ((), (), s32[]{:S(2)}) async-start(), calls=%async_computation.3 | async-start | bytes 3244032 | tf_op jit(solution)/shard_map/all_gather | solution.py:77
  9.4 235.0 %all-gather.9.cloned.1.call-start = ((), (), s32[]{:S(2)}) async-start(), calls=%async_computation.4 | async-start | bytes 5308416 | tf_op jit(solution)/shard_map/all_gather | solution.py:85
  10.0 350.0 %all-gather.15.cloned.1.call-start = ((), (), s32[]{:S(2)}) async-start(), calls=%async_computation.7 | async-start | bytes 1769472 | tf_op jit(solution)/shard_map/all_gather | solution.py:101
  250.3 140.2 %all-gather.17.cloned.1.call-start = ((), (), s32[]{:S(2)}) async-start(), calls=%async_computation.8 | async-start | bytes 1769472 | tf_op jit(solution)/shard_map/all_gather | solution.py:102
  250.9 296.1 %reduce-scatter.4.cloned.1.call-start = ((), (), s32[]{:S(2)}) async-start(), calls=%async_computation.9 | async-start | bytes 6488064
  264.5 1.9 copy-start
  316.1 41.0 %all-to-all-start.1 = ((bf16[256,8,768]{0,2,1:T(8,128)(2,1)}), bf16[256,8,768]{0,2,1:T(8,128)(2,1)S(1)}, u32[]{:S(2)}, u32[]{:S(2)}) async-start(bf16[256,8,768]{0,2,1:T(8,128)(2,1)} %bitcast.39), calls=%async_computation.1 | async-start | bytes 6291456 | tf_op jit(solution)/shard_map/all_to_all | solution.py:81
  320.2 4.3 copy-start.8
  325.5 2.7 copy-start.9
  332.0 4.3 copy-start.10
  337.4 2.7 copy-start.11
  370.4 1.6 copy-start.5
  384.0 6.5 %copy-start.1 = (bf16[8,256,768]{2,1,0:T(8,128)(2,1)S(1)}, bf16[8,256,768]{2,1,0:T(8,128)(2,1)}, u32[]{:S(2)}) copy-start(bf16[8,256,768]{2,1,0:T(8,128)(2,1)} %copy.109) | copy-start | bytes 9437188
  398.5 1.3 copy-start.4
  402.5 2.9 copy-start.2
  402.5 2.9 copy-start.3
  408.9 2.2 copy-start.7
  408.9 3.3 copy-start.6
Sparse Core Ops, SparseCore 0:
  10.6 82.2 all-gather.10
  94.7 32.4 all-gather.12
  129.8 80.3 all-gather.6
  211.9 32.4 all-gather.8
  250.4 27.9 all-gather.14
  280.1 34.5 all-gather.16
  318.7 228.2 reduce-scatter.3
where the time goes:
time: 557 us; the launch traced here: 556 us
  waiting for transfers between devices  370 us (66%)
  local copies, waits for them, and re-layouts  75.1 us (13%)
  blocking collectives  49.7 us (9%)
  matrix products  31.3 us (6%)
  between operations  14.2 us (3%)
  other arithmetic  11.2 us (2%)
    unnamed x8, waiting for transfers between devices  137 us
    all_gather x1, waiting for transfers between devices, local(): lax.all_gather(tokens, 'col', axis=1, tiled=True)  82.9 us
    all_gather x1, waiting for transfers between devices, local(): lax.all_gather(cotangent, 'col', axis=1, tiled=True)  77.2 us
    all_to_all x1, blocking collectives, local(): lax.all_to_all(token_rows, 'row', split_axis=1, concat_axis=0, tiled=True)  49.7 us
    unnamed x39, local copies, waits for them, and re-layouts  35.3 us
    all_gather x1, waiting for transfers between devices, local(): lax.all_gather(w_expand, 'row', axis=0, tiled=True)  34.3 us
    all_gather x1, waiting for transfers between devices, local(): lax.all_gather(w_reduce, 'row', axis=0, tiled=True)  34.2 us
    mul x16, local copies, waits for them, and re-layouts, spread_scale(): return (shaped * scale[:, None, :]).reshape(values.shape)  26.2 us
  transfers between devices with their start and end apart: 8, of which 6 were waited for; matrix products, arithmetic and copies ran while one was open for 19% of the time, Pallas kernels for 0%

commit v1 on v0

--- a/solution.py
+++ b/solution.py
@@ -74,7 +74,7 @@
 ):
     token_rows, cot_rows = (
         lax.all_gather(tokens, "col", axis=1, tiled=True),
-        lax.all_gather(cotangent, "col", axis=1, tiled=True),
+        jnp.concatenate(lax.all_gather(cotangent, "col"), axis=1),
     )
     input_whole, cot_whole = (
         lax.all_to_all(token_rows, "row", split_axis=1, concat_axis=0, tiled=True),

time: 557 us -> 559 us (level)
  local copies, waits for them, and re-layouts: 75.1 us -> 81.4 us
    all_gather x1, waiting for transfers between devices: 82.9 us -> 75.4 us  [local(): lax.all_gather(tokens, 'col', axis=1, tiled=True)]
    unnamed x39 -> x40, local copies, waits for them, and re-layouts: 35.3 us -> 38.1 us
  transfers between devices with their start and end apart: 8 -> 8, of which waited for: 6 -> 6; matrix products, arithmetic and copies ran while one was open for 19% -> 20% of each run, Pallas kernels for 0% -> 0%
where the time goes in v1:
time: 559 us; the launch traced here: 558 us
  waiting for transfers between devices  365 us (65%)
  local copies, waits for them, and re-layouts  81.4 us (15%)
  blocking collectives  49.7 us (9%)
  matrix products  31.3 us (6%)
  between operations  14.2 us (3%)
  other arithmetic  11.2 us (2%)
    unnamed x8, waiting for transfers between devices  137 us
    all_gather x1, waiting for transfers between devices, local(): lax.all_gather(cotangent, 'col')  82 us
    all_gather x1, waiting for transfers between devices, local(): lax.all_gather(tokens, 'col', axis=1, tiled=True)  75.4 us
    all_to_all x1, blocking collectives, local(): lax.all_to_all(token_rows, 'row', split_axis=1, concat_axis=0, tiled=True)  49.7 us
    unnamed x40, local copies, waits for them, and re-layouts  38.1 us
    all_gather x1, waiting for transfers between devices, local(): lax.all_gather(w_expand, 'row', axis=0, tiled=True)  34.3 us
    all_gather x1, waiting for transfers between devices, local(): lax.all_gather(w_reduce, 'row', axis=0, tiled=True)  32.7 us
    mul x16, local copies, waits for them, and re-layouts, spread_scale(): return (shaped * scale[:, None, :]).reshape(values.shape)  26.3 us
  transfers between devices with their start and end apart: 8, of which 6 were waited for; matrix products, arithmetic and copies ran while one was open for 20% of the time, Pallas kernels for 0%

profile of v1, /device:TPU:8, one launch (start us, length us, event | category | flops | bytes accessed | tf_op | source)
XLA Modules:
  0.0 557.6 jit_solution(6786839672458838422)
XLA Ops:
  10.0 82.0 %all-gather.18.cloned.1.call-done = bf16[8192,192]{0,1:T(8,128)(2,1)} async-done(((bf16[256,192]{0,1:T(8,128)(2,1)}), bf16[8192,192]{0,1:T(8,128)(2,1)}) %all-gather.18.cloned.1.call-update) | async-done | bytes 3145744 | tf_op jit(solution)/shard_map/all_gather | solution.py:77
  92.0 2.8 copy.130
  94.9 3.4 copy.99
  98.3 75.4 %all-gather.10.cloned.1.call-done = bf16[256,6144]{0,1:T(8,128)(2,1)} async-done(((bf16[256,192]{0,1:T(8,128)(2,1)}), bf16[256,6144]{0,1:T(8,128)(2,1)}) %all-gather.10.cloned.1.call-update) | async-done | bytes 3145744 | tf_op jit(solution)/shard_map/all_gather | solution.py:76
  173.7 34.3 %all-gather.12.cloned.1.call-done = bf16[6144,384]{1,0:T(8,128)(2,1)} async-done(((bf16[768,384]{1,0:T(8,128)(2,1)}), bf16[6144,384]{1,0:T(8,128)(2,1)}) %all-gather.12.cloned.1.call-update) | async-done | bytes 4718608 | tf_op jit(solution)/shard_map/all_gather | solution.py:84
  208.0 5.8 %multiply_convert_fusion.4 = (bf16[256,384]{1,0:T(8,128)(2,1)}, f32[256,384]{1,0:T(8,128)S(1)}) fusion(bf16[256,6144]{0,1:T(8,128)(2,1)} %all-gather.10.cloned.1.call-done, bf16[6144,384]{1,0:T(8,128)(2,1)} %all-gather.12.cloned.1.call-done), kind=kOutput, calls=%fused_computation.30 | convolution fusion | flops 1208451072 | bytes 8454144 | tf_op jit(solution)/shard_map/dot_general | solution.py:87
  213.9 32.7 %all-gather.8.cloned.1.call-done = bf16[6144,384]{1,0:T(8,128)(2,1)} async-done(((bf16[768,384]{1,0:T(8,128)(2,1)}), bf16[6144,384]{1,0:T(8,128)(2,1)}) %all-gather.8.cloned.1.call-update) | async-done | bytes 4718608 | tf_op jit(solution)/shard_map/all_gather | solution.py:85
  246.5 5.8 %fusion.8 = bf16[256,384]{1,0:T(8,128)(2,1)} fusion(bf16[256,6144]{0,1:T(8,128)(2,1)} %bitcast.1, bf16[6144,384]{1,0:T(8,128)(2,1)} %all-gather.8.cloned.1.call-done, f32[256,384]{1,0:T(8,128)S(1)} %get-tuple-element.82), kind=kOutput, calls=%fused_computation.24 | convolution fusion | flops 1208942592 | bytes 8454144 | tf_op jit(solution)/shard_map/dot_general | solution.py:88
  253.0 7.0 %convolution_bitcast_fusion = f32[6144,256]{0,1:T(8,128)} fusion(bf16[256,384]{1,0:T(8,128)(2,1)} %fusion.8, bf16[6144,384]{1,0:T(8,128)(2,1)} %all-gather.12.cloned.1.call-done), kind=kOutput, calls=%fused_computation | convolution fusion | flops 1207959552 | bytes 11206656 | tf_op jit(solution)/shard_map/dot_general | solution.py:93
  260.0 6.6 %copy.128 = f32[6144,256]{1,0:T(8,128)} copy(f32[6144,256]{0,1:T(8,128)} %convolution_bitcast_fusion) | data formatting | bytes 12582912
  268.5 49.7 %all_to_all.38 = bf16[256,8,768]{0,2,1:T(8,128)(2,1)} all-to-all(bf16[256,8,768]{0,2,1:T(8,128)(2,1)S(1)} %bitcast.45), channel_id=1, replica_groups=mesh['row'=8,'col'=32] {'row'}, dimensions={1} | all-to-all | bytes 6291456 | tf_op jit(solution)/shard_map/all_to_all | solution.py:80
  318.2 4.0 all-to-all-start.1
  322.3 2.1 copy.100
  327.6 2.7 copy.102
  331.4 2.7 copy.105
  334.1 2.1 copy.101
  339.5 2.7 copy.112
  343.3 2.7 copy.116
  345.9 2.1 copy.111
  350.2 4.7 copy.103
  354.9 4.3 all-to-all-done.1
  359.3 2.8 copy.114
  362.0 6.3 %fusion.18 = (f32[768,384]{0,1:T(8,128)}, f32[768,384]{0,1:T(8,128)S(1)}, f32[768,384]{0,1:T(8,128)S(1)}, f32[768,384]{0,1:T(8,128)S(1)}) fusion(f32[768,384]{0,1:T(8,128)} %copy.102, bf16[768,384]{0,1:T(8,128)(2,1)} %copy.101, f32[768,384]{0,1:T(8,128)} %copy.105, bf16[768,384]{0,1:T(8,128)(2,1)} %copy.104, ...), kind=kOutput, calls=%fused_computation.44 | convolution fusion | flops 1211793408 | bytes 12976128 | tf_op jit(solution)/shard_map/dot_general | solution.py:56
  368.3 2.7 copy.106
  380.0 2.7 copy.109
  382.7 3.5 multiply_convert_fusion.2
  386.2 2.3 copy.122
  392.7 6.4 %fusion.15 = (f32[768,384]{0,1:T(8,128)}, f32[768,384]{0,1:T(8,128)}, f32[768,384]{0,1:T(8,128)}, f32[768,384]{0,1:T(8,128)}) fusion(f32[768,384]{0,1:T(8,128)} %copy.112, bf16[768,384]{0,1:T(8,128)(2,1)} %copy.111, f32[768,384]{0,1:T(8,128)} %copy.116, bf16[768,384]{0,1:T(8,128)(2,1)} %copy.115, bf16[2048,384]{1,0:T(8,128)(2,1)} %all-gather.16.cloned.1.call-done, ...), kind=kOutput, calls=%fused_computation.42 | convolution fusion | flops 1211793408 | bytes 12976128 | tf_op jit(solution)/shard_map/dot_general | solution.py:56
  404.8 2.9 copy.120
  407.6 3.5 multiply_convert_fusion
  411.2 2.2 copy.125
  415.5 133.5 %reduce-scatter.4.cloned.1.call-done = f32[192,256]{1,0:T(8,128)} async-done(((f32[6144,256]{1,0:T(8,128)}), f32[192,256]{1,0:T(8,128)}) %reduce-scatter.4.cloned.1.call-update) | async-done | bytes 196624
  (68 shorter events, 38.8 us)
Async XLA Ops:
  7.2 84.9 %all-gather.18.cloned.1.call-start = ((), (), s32[]{:S(2)}) async-start(), calls=%async_computation.8 | async-start | bytes 3244032 | tf_op jit(solution)/shard_map/all_gather | solution.py:77
  7.9 165.8 %all-gather.10.cloned.1.call-start = ((), (), s32[]{:S(2)}) async-start(), calls=%async_computation.4 | async-start | bytes 3244032 | tf_op jit(solution)/shard_map/all_gather | solution.py:76
  8.7 199.4 %all-gather.12.cloned.1.call-start = ((), (), s32[]{:S(2)}) async-start(), calls=%async_computation.5 | async-start | bytes 5308416 | tf_op jit(solution)/shard_map/all_gather | solution.py:84
  9.4 237.2 %all-gather.8.cloned.1.call-start = ((), (), s32[]{:S(2)}) async-start(), calls=%async_computation.3 | async-start | bytes 5308416 | tf_op jit(solution)/shard_map/all_gather | solution.py:85
  10.0 352.1 %all-gather.14.cloned.1.call-start = ((), (), s32[]{:S(2)}) async-start(), calls=%async_computation.6 | async-start | bytes 1769472 | tf_op jit(solution)/shard_map/all_gather | solution.py:101
  252.4 140.3 %all-gather.16.cloned.1.call-start = ((), (), s32[]{:S(2)}) async-start(), calls=%async_computation.7 | async-start | bytes 1769472 | tf_op jit(solution)/shard_map/all_gather | solution.py:102
  253.0 296.0 %reduce-scatter.4.cloned.1.call-start = ((), (), s32[]{:S(2)}) async-start(), calls=%async_computation.9 | async-start | bytes 6488064
  266.6 1.9 copy-start
  318.2 41.0 %all-to-all-start.1 = ((bf16[256,8,768]{0,2,1:T(8,128)(2,1)}), bf16[256,8,768]{0,2,1:T(8,128)(2,1)S(1)}, u32[]{:S(2)}, u32[]{:S(2)}) async-start(bf16[256,8,768]{0,2,1:T(8,128)(2,1)} %bitcast.15), calls=%async_computation.1 | async-start | bytes 6291456 | tf_op jit(solution)/shard_map/all_to_all | solution.py:81
  322.3 4.3 copy-start.8
  327.6 2.7 copy-start.9
  334.1 4.3 copy-start.10
  339.5 2.7 copy-start.11
  372.5 1.6 copy-start.5
  386.2 6.5 %copy-start.1 = (bf16[8,256,768]{2,1,0:T(8,128)(2,1)S(1)}, bf16[8,256,768]{2,1,0:T(8,128)(2,1)}, u32[]{:S(2)}) copy-start(bf16[8,256,768]{2,1,0:T(8,128)(2,1)} %copy.114) | copy-start | bytes 9437188
  400.8 1.3 copy-start.4
  404.7 2.9 copy-start.2
  404.8 2.9 copy-start.3
  411.2 2.2 copy-start.7
  411.2 3.3 copy-start.6
Sparse Core Ops, SparseCore 0:
  10.4 81.5 all-gather.17
  94.6 78.9 all-gather.9
  175.5 32.4 all-gather.11
  209.7 36.8 all-gather.7
  252.5 27.9 all-gather.13
  282.2 34.5 all-gather.15
  320.8 228.1 reduce-scatter.3
